TPU v7x, 128 devices: a whole 4x4x4 slice. The times are simulated.
128 devices in a mesh: sens: 8 (over z, core), layer: 16 (over y, x).
Axes of the slice: x: 4, y: 4, z: 4, core: 2. Of those that a mesh axis runs over, the one named last changes fastest.
Arguments:
- slopes: bfloat16 [1024, 63600], P('layer', 'sens'), may hold values from -7 to 7
- valid: int32 [63600], P('sens'), may hold values from 0 to 1
- sensor_map: int32 [63600], P('sens'), may hold values from 0 to 5, as said below
- reconstructor: bfloat16 [16000, 63600], P('layer', 'sens'), may hold values from -0.0234375 to 0.0234375
- fitting: bfloat16 [7800, 16000], P('sens', 'layer'), may hold values from -0.046875 to 0.046875
Outputs:
- commands: float32 [1024, 7800], P(('sens', 'layer'))
Inputs may be any that keep to these rules, and one draw needn't show every extreme that they name: `sensor_map`: both slopes of a subaperture (indices 2 i and 2 i + 1) belong to one sensor.
All inputs are finite; a program needn't handle non-finite values.
Results may differ from a plain program's by a relative error of at most 0.02.
Values may be sent and summed in bfloat16 or wider, within the bound.
No kernel may reach another device: no remote copies, remote signals or barrier semaphores. Data moves between devices by JAX's collectives and lax.ppermute only.
A program may use at most 192 MiB of HBM per device.

v0:
```python
import jax
import jax.numpy as jnp
from jax import lax
from jax.sharding import PartitionSpec as P

SENSORS = 6


def copy_for_each(x, axis):
    length = lax.axis_size(axis)
    return lax.all_to_all(jnp.broadcast_to(x[None], (length, *x.shape)), axis, 0, 0, tiled=True)


def taken_together(x, axis):
    everything = copy_for_each(x, axis)
    return jnp.sum(everything.astype(jnp.float32), axis=0)


def cut_along(x, dim, length):
    dims = x.shape
    blocks = x.reshape(*dims[:dim], length, dims[dim] // length, *dims[dim + 1 :])
    return jnp.moveaxis(blocks, dim, 0)


def summed_on_arrival(x, axis, dim):
    blocks = cut_along(x, dim, lax.axis_size(axis))
    arrived = lax.all_to_all(blocks, axis, split_axis=0, concat_axis=0, tiled=True)
    return arrived.astype(jnp.float32).sum(axis=0)


def contract(left, right):
    return lax.dot_general(
        left, right, (((1,), (1,)), ((), ())), preferred_element_type=jnp.float32
    )


def cleaned(block, live, onehot_full, sums, counts):
    means = sums / jnp.maximum(counts, 1.0)
    spread = lax.dot_general(
        means, onehot_full, (((1,), (1,)), ((), ())), precision=lax.Precision.HIGHEST
    )
    return (live.astype(jnp.float32)[None, :] * (block.astype(jnp.float32) - spread)).astype(
        jnp.bfloat16
    )


def per_device(slopes, valid, sensor_map, reconstructor, fitting):
    width_local = slopes.shape[1]
    start = lax.axis_index("sens") * width_local
    parity = (lax.iota(jnp.int32, width_local) + start) % 2
    group = sensor_map * 2 + parity
    labels = lax.iota(jnp.int32, 2 * SENSORS)
    onehot_full = (group[:, None] == labels[None, :]).astype(jnp.float32)
    onehot_low = onehot_full.astype(jnp.bfloat16)
    live = valid.astype(jnp.bfloat16)
    count_terms = jnp.dot(live[None, :], onehot_low, preferred_element_type=jnp.float32)[0]
    whole = lax.all_gather(slopes, "layer", axis=0, tiled=True)
    masked = whole * live[None, :]
    sums = jnp.dot(masked, onehot_low, preferred_element_type=jnp.float32)
    sums, counts = (
        taken_together(sums.astype(jnp.bfloat16), "sens").astype(jnp.float32),
        taken_together(count_terms.astype(jnp.bfloat16), "sens").astype(jnp.float32),
    )
    clean = cleaned(whole, live, onehot_full, sums, counts)
    partial_points = contract(clean, reconstructor)
    points = summed_on_arrival(partial_points.astype(jnp.bfloat16), "sens", 0).astype(jnp.bfloat16)
    partial_commands = contract(points, lax.all_gather(fitting, "sens", axis=0, tiled=True))
    return summed_on_arrival(partial_commands.astype(jnp.bfloat16), "layer", 0)


def solution(mesh):
    placed = (P("layer", "sens"), P("sens"), P("sens"), P("layer", "sens"), P("sens", "layer"))
    return jax.shard_map(
        per_device,
        mesh=mesh,
        in_specs=placed,
        out_specs=P(("sens", "layer"), None),
        check_vma=False,
    )
```

profile of v0, /device:TPU:0, one launch (start us, length us, event | category | flops | bytes accessed | tf_op | source)
XLA Modules:
  0.0 284.0 jit_solution(14590893099064575598)
XLA Ops:
  6.5 0.0 all-gather.4.cloned.1.call-start
  6.5 0.7 all-gather.4.cloned.1.call-update
  7.3 0.0 all-gather.6.cloned.1.call-start
  7.3 0.7 all-gather.6.cloned.1.call-update
  8.0 0.8 fusion.17
  8.8 0.2 fusion.6
  9.0 10.5 %all_to_all.21 = bf16[8,1,12]{2,1,0:T(2,128)(2,1)S(1)} all-to-all(bf16[8,1,12]{2,1,0:T(2,128)(2,1)S(1)} %broadcast_in_dim.5), channel_id=1, replica_groups=mesh['sens'=8,'layer'=16] {'sens'}, dimensions={0} | all-to-all | bytes 384 | tf_op jit(solution)/shard_map/all_to_all | solution.py:11
  19.5 102.3 %all-gather.4.cloned.1.call-done = bf16[1024,7950]{1,0:T(8,128)(2,1)} async-done(((bf16[64,7950]{1,0:T(8,128)(2,1)}), bf16[1024,7950]{1,0:T(8,128)(2,1)}) %all-gather.4.cloned.1.call-update) | async-done | bytes 16281616 | tf_op jit(solution)/shard_map/all_gather | solution.py:57
  121.9 10.0 %fusion.3 = bf16[1024,12]{0,1:T(8,128)(2,1)S(1)} fusion(bf16[1024,7950]{1,0:T(8,128)(2,1)} %all-gather.4.cloned.1.call-done, bf16[7950]{0:T(1024)(128)(2,1)S(1)} %get-tuple-element.6, s32[7950]{0:T(1024)S(1)} %get-tuple-element.7), kind=kOutput, calls=%fused_computation.8 | convolution fusion | flops 203818496 | bytes 16353876 | tf_op jit(solution)/shard_map/dot_general | solution.py:59
  131.9 0.8 broadcast_in_dim.4
  132.7 4.4 %all-to-all-start = ((bf16[8,1024,12]{1,2,0:T(8,128)(2,1)}), bf16[8,1024,12]{1,2,0:T(8,128)(2,1)S(1)}, u32[]{:S(2)}, u32[]{:S(2)}) async-start(bf16[8,1024,12]{1,2,0:T(8,128)(2,1)} %broadcast_in_dim.4), calls=%async_computation | async-start | bytes 524288 | tf_op jit(solution)/shard_map/all_to_all | solution.py:11
  137.1 22.4 %copy.24 = bf16[1024,7950]{0,1:T(8,128)(2,1)} copy(bf16[1024,7950]{1,0:T(8,128)(2,1)} %all-gather.4.cloned.1.call-done) | data formatting | bytes 32563200 | tf_op jit(solution)/shard_map/all_gather | solution.py:57
  159.5 0.0 all-to-all-done
  159.6 19.0 %multiply_convert_fusion = bf16[1024,7950]{0,1:T(8,128)(2,1)S(1)} fusion(bf16[1024,7950]{0,1:T(8,128)(2,1)} %copy.24, f32[7950]{0:T(1024)S(1)} %get-tuple-element.5, s32[7950]{0:T(1024)S(1)} %get-tuple-element.7, f32[1024,12]{0,1:T(8,128)S(1)} %convert_reduce_fusion.1, f32[12]{0:T(128)S(1)} %broadcast_maximum_fusion), kind=kOutput, calls=%fused_computation | convolution fusion | flops 1204946048 | bytes 32676000 | tf_op jit(solution)/shard_map/dot_general | solution.py:39
  178.5 20.7 %convert_bitcast_fusion = bf16[125,8,8,128]{3,2,1,0:T(8,128)(2,1)S(1)} fusion(bf16[1024,7950]{0,1:T(8,128)(2,1)S(1)} %multiply_convert_fusion, bf16[1000,7950]{1,0:T(8,128)(2,1)} %param.8), kind=kOutput, calls=%fused_computation.7 | convolution fusion | flops 16282624000 | bytes 34229600 | tf_op jit(solution)/shard_map/dot_general | solution.py:32
  199.3 1.6 copy.33
  200.9 4.7 %all-to-all-start.2 = ((bf16[8,128,1000]{1,2,0:T(8,128)(2,1)}), bf16[8,128,1000]{1,2,0:T(8,128)(2,1)S(1)}, u32[]{:S(2)}, u32[]{:S(2)}) async-start(bf16[8,128,1000]{1,2,0:T(8,128)(2,1)} %bitcast.16), calls=%async_computation.2 | async-start | bytes 4096000 | tf_op jit(solution)/shard_map/all_to_all | solution.py:27
  205.7 2.3 all-gather.6.cloned.1.call-done
  208.0 20.5 %reshape.30 = bf16[7800,1000]{1,0:T(8,128)(2,1)} reshape(bf16[8,975,1000]{2,1,0:T(8,128)(2,1)} %all-gather.6.cloned.1.call-done) | data formatting | bytes 31200000
  228.5 3.8 %all-to-all-done.2 = bf16[8,128,1000]{1,2,0:T(8,128)(2,1)S(1)} async-done(((bf16[8,128,1000]{1,2,0:T(8,128)(2,1)}), bf16[8,128,1000]{1,2,0:T(8,128)(2,1)S(1)}, u32[]{:S(2)}, u32[]{:S(2)}) %all-to-all-start.2) | async-done | bytes 2048032 | tf_op jit(solution)/shard_map/all_to_all | solution.py:27
  232.3 0.4 reduce_sum.41
  232.7 9.3 %convolution_convert_fusion = bf16[128,7800]{0,1:T(8,128)(2,1)} fusion(bf16[128,1000]{0,1:T(8,128)(2,1)S(1)} %reduce_sum.41, bf16[7800,1000]{1,0:T(8,128)(2,1)} %reshape.30), kind=kOutput, calls=%fused_computation.3 | convolution fusion | flops 1997798400 | bytes 17852800 | tf_op jit(solution)/shard_map/dot_general | solution.py:32
  242.0 2.9 %copy.28 = bf16[128,7800]{1,0:T(8,128)(2,1)S(1)} copy(bf16[128,7800]{0,1:T(8,128)(2,1)} %convolution_convert_fusion) | data formatting | bytes 3993600 | tf_op jit(solution)/shard_map/convert_element_type | solution.py:68
  244.9 31.2 %all_to_all.22 = bf16[16,8,7800]{2,1,0:T(8,128)(2,1)S(1)} all-to-all(bf16[16,8,7800]{2,1,0:T(8,128)(2,1)S(1)} %bitcast.17), channel_id=1, replica_groups=mesh['sens'=8,'layer'=16] {'layer'}, dimensions={0} | all-to-all | bytes 3993600 | tf_op jit(solution)/shard_map/all_to_all | solution.py:27
  276.2 1.0 convert_reduce_fusion
  (5 shorter events, 0.1 us)
Async XLA Ops:
  6.5 115.3 %all-gather.4.cloned.1.call-start = ((), (), s32[]{:S(2)}) async-start(), calls=%async_computation.4 | async-start | bytes 17547264 | tf_op jit(solution)/shard_map/all_gather | solution.py:57
  7.3 200.7 %all-gather.6.cloned.1.call-start = ((), (), s32[]{:S(2)}) async-start(), calls=%async_computation.5 | async-start | bytes 17989632 | tf_op jit(solution)/shard_map/all_gather | solution.py:67
  132.7 26.8 %all-to-all-start = ((bf16[8,1024,12]{1,2,0:T(8,128)(2,1)}), bf16[8,1024,12]{1,2,0:T(8,128)(2,1)S(1)}, u32[]{:S(2)}, u32[]{:S(2)}) async-start(bf16[8,1024,12]{1,2,0:T(8,128)(2,1)} %broadcast_in_dim.4), calls=%async_computation | async-start | bytes 524288 | tf_op jit(solution)/shard_map/all_to_all | solution.py:11
  200.9 31.4 %all-to-all-start.2 = ((bf16[8,128,1000]{1,2,0:T(8,128)(2,1)}), bf16[8,128,1000]{1,2,0:T(8,128)(2,1)S(1)}, u32[]{:S(2)}, u32[]{:S(2)}) async-start(bf16[8,128,1000]{1,2,0:T(8,128)(2,1)} %bitcast.16), calls=%async_computation.2 | async-start | bytes 4096000 | tf_op jit(solution)/shard_map/all_to_all | solution.py:27
Sparse Core Ops, SparseCore 0:
  9.5 112.3 all-gather.3
  123.5 84.3 all-gather.5
where the time goes:
time: 285 us; the launch traced here: 284 us
  waiting for transfers between devices  110 us (39%)
  matrix products  59.2 us (21%)
  local copies, waits for them, and re-layouts  48.3 us (17%)
  blocking collectives  41.7 us (15%)
  between operations  13.5 us (5%)
  starting transfers between devices  9.2 us (3%)
    all_gather x1, waiting for transfers between devices, per_device(): whole = lax.all_gather(slopes, 'layer', axis=0, tiled=True)  102 us
    all_to_all x1, blocking collectives, summed_on_arrival(): lax.all_to_all(blocks, axis, split_axis=0, concat_axis=0, tiled=True)  31.2 us
    dot_general x2, matrix products, contract(): lax.dot_general(left, right, (((1,), (1,)), ((), ())), preferred_element_...  30 us
    all_gather x1, local copies, waits for them, and re-layouts, per_device(): whole = lax.all_gather(slopes, 'layer', axis=0, tiled=True)  22.4 us
    unnamed x1, local copies, waits for them, and re-layouts  20.5 us
    dot_general x1, matrix products, cleaned(): lax.dot_general(means, onehot_full, (((1,), (1,)), ((), ())), precision=l...  19 us
    all_to_all x1, blocking collectives, copy_for_each(): lax.all_to_all(jnp.broadcast_to(x[None], (length, *x.shape)), axis, 0, 0,...  10.5 us
    dot_general x1, matrix products, per_device(): sums = jnp.dot(masked, onehot_low, preferred_element_type=jnp.float32)  10 us
  transfers between devices with their start and end apart: 4, of which 3 were waited for; matrix products, arithmetic and copies ran while one was open for 34% of the time, Pallas kernels for 0%

commit v1 on v0

--- a/solution.py
+++ b/solution.py
@@ -54,7 +54,8 @@
     onehot_low = onehot_full.astype(jnp.bfloat16)
     live = valid.astype(jnp.bfloat16)
     count_terms = jnp.dot(live[None, :], onehot_low, preferred_element_type=jnp.float32)[0]
-    whole = lax.all_gather(slopes, "layer", axis=0, tiled=True)
+    sent = jnp.stack([slopes] * lax.axis_size("layer"))
+    whole = jnp.concatenate(lax.all_to_all(sent, "layer", 0, 0), axis=0)
     masked = whole * live[None, :]
     sums = jnp.dot(masked, onehot_low, preferred_element_type=jnp.float32)
     sums, counts = (

time: 285 us -> 461 us (1.62)
  waiting for transfers between devices: 110 us -> 247 us
  blocking collectives: 41.7 us -> 71.7 us
  local copies, waits for them, and re-layouts: 48.3 us -> 55.7 us
    all_to_all x1, waiting for transfers between devices: 3.81 us -> 246 us  [per_device(): whole = jnp.concatenate(lax.all_to_all(sent, 'layer', 0, 0), axis=0)]
    all_gather x1 -> x0, waiting for transfers between devices: 102 us -> none  [per_device(): whole = lax.all_gather(slopes, 'layer', axis=0, tiled=True)]
    all_to_all x1 -> x2, blocking collectives: 31.2 us -> 61.3 us  [summed_on_arrival(): lax.all_to_all(blocks, axis, split_axis=0, concat_axis=0, tiled=True)]
    all_gather x1 -> x0, local copies, waits for them, and re-layouts: 22.4 us -> none  [per_device(): whole = lax.all_gather(slopes, 'layer', axis=0, tiled=True)]
    reshape x0 -> x1, local copies, waits for them, and re-layouts: none -> 22.2 us  [per_device(): whole = jnp.concatenate(lax.all_to_all(sent, 'layer', 0, 0), axis=0)]
    another operation x0 -> x1, local copies, waits for them, and re-layouts: none -> 8.79 us  [per_device(): sent = jnp.stack([slopes] * lax.axis_size('layer'))]
  transfers between devices with their start and end apart: 4 -> 3, of which waited for: 3 -> 1; matrix products, arithmetic and copies ran while one was open for 34% -> 18% of each run, Pallas kernels for 0% -> 0%
where the time goes in v1:
time: 461 us; the launch traced here: 460 us
  waiting for transfers between devices  247 us (54%)
  blocking collectives  71.7 us (16%)
  matrix products  58.9 us (13%)
  local copies, waits for them, and re-layouts  55.7 us (12%)
  between operations  13.5 us (3%)
  starting transfers between devices  10.6 us (2%)
    all_to_all x1, waiting for transfers between devices, per_device(): whole = jnp.concatenate(lax.all_to_all(sent, 'layer', 0, 0), axis=0)  246 us
    all_to_all x2, blocking collectives, summed_on_arrival(): lax.all_to_all(blocks, axis, split_axis=0, concat_axis=0, tiled=True)  61.3 us
    dot_general x2, matrix products, contract(): lax.dot_general(left, right, (((1,), (1,)), ((), ())), preferred_element_...  29.8 us
    reshape x1, local copies, waits for them, and re-layouts, per_device(): whole = jnp.concatenate(lax.all_to_all(sent, 'layer', 0, 0), axis=0)  22.2 us
    unnamed x1, local copies, waits for them, and re-layouts  20.6 us
    dot_general x1, matrix products, cleaned(): lax.dot_general(means, onehot_full, (((1,), (1,)), ((), ())), precision=l...  18.9 us
    all_to_all x1, blocking collectives, copy_for_each(): lax.all_to_all(jnp.broadcast_to(x[None], (length, *x.shape)), axis, 0, 0,...  10.5 us
    dot_general x1, matrix products, per_device(): sums = jnp.dot(masked, onehot_low, preferred_element_type=jnp.float32)  10 us
  transfers between devices with their start and end apart: 3, of which 1 were waited for; matrix products, arithmetic and copies ran while one was open for 18% of the time, Pallas kernels for 0%

profile of v1, /device:TPU:0, one launch (start us, length us, event | category | flops | bytes accessed | tf_op | source)
XLA Modules:
  0.0 459.7 jit_solution(1127645338708991922)
XLA Ops:
  6.5 0.0 all-gather.3.cloned.1.call-start
  6.5 0.7 all-gather.3.cloned.1.call-update
  7.3 0.8 fusion.17
  8.1 0.2 fusion.6
  8.3 10.5 %all_to_all.26 = bf16[8,1,12]{2,1,0:T(2,128)(2,1)S(1)} all-to-all(bf16[8,1,12]{2,1,0:T(2,128)(2,1)S(1)} %broadcast_in_dim.5), channel_id=1, replica_groups=mesh['sens'=8,'layer'=16] {'sens'}, dimensions={0} | all-to-all | bytes 384 | tf_op jit(solution)/shard_map/all_to_all | solution.py:11
  18.8 8.8 %stack.2 = bf16[16,64,7950]{2,1,0:T(8,128)(2,1)} broadcast(bf16[64,7950]{1,0:T(8,128)(2,1)} %param.5), dimensions={1,2} | broadcast | bytes 17299200 | tf_op jit(solution)/shard_map/stack | solution.py:57
  27.6 7.0 %all-to-all-start = ((bf16[16,64,7950]{2,1,0:T(8,128)(2,1)}), bf16[16,64,7950]{2,1,0:T(8,128)(2,1)}, u32[]{:S(2)}, u32[]{:S(2)}) async-start(bf16[16,64,7950]{2,1,0:T(8,128)(2,1)} %stack.2), calls=%async_computation | async-start | bytes 33030144 | tf_op jit(solution)/shard_map/all_to_all | solution.py:58
  34.6 246.4 %all-to-all-done = bf16[16,64,7950]{2,1,0:T(8,128)(2,1)} async-done(((bf16[16,64,7950]{2,1,0:T(8,128)(2,1)}), bf16[16,64,7950]{2,1,0:T(8,128)(2,1)}, u32[]{:S(2)}, u32[]{:S(2)}) %all-to-all-start) | async-done | bytes 16281632 | tf_op jit(solution)/shard_map/all_to_all | solution.py:58
  281.0 10.0 %fusion.3 = bf16[1024,12]{0,1:T(8,128)(2,1)S(1)} fusion(bf16[1024,7950]{1,0:T(8,128)(2,1)} %bitcast, bf16[7950]{0:T(1024)(128)(2,1)S(1)} %get-tuple-element.6, s32[7950]{0:T(1024)S(1)} %get-tuple-element.7), kind=kOutput, calls=%fused_computation.8 | convolution fusion | flops 203818496 | bytes 16353876 | tf_op jit(solution)/shard_map/dot_general | solution.py:60
  291.0 0.8 broadcast_in_dim.4
  291.8 3.6 all-to-all-start.1
  295.4 22.2 %copy.28 = bf16[1024,7950]{0,1:T(8,128)(2,1)} copy(bf16[1024,7950]{1,0:T(8,128)(2,1)} %bitcast) | data formatting | bytes 32563200 | tf_op jit(solution)/shard_map/reshape | solution.py:58
  317.6 0.0 all-to-all-done.1
  317.7 18.9 %multiply_convert_fusion = bf16[1024,7950]{0,1:T(8,128)(2,1)S(1)} fusion(bf16[1024,7950]{0,1:T(8,128)(2,1)} %copy.28, f32[7950]{0:T(1024)S(1)} %get-tuple-element.5, s32[7950]{0:T(1024)S(1)} %get-tuple-element.7, f32[1024,12]{0,1:T(8,128)S(1)} %convert_reduce_fusion.1, f32[12]{0:T(128)S(1)} %broadcast_maximum_fusion), kind=kOutput, calls=%fused_computation | convolution fusion | flops 1204946048 | bytes 32676000 | tf_op jit(solution)/shard_map/dot_general | solution.py:39
  336.6 20.5 %convert_bitcast_fusion = bf16[125,8,8,128]{3,2,1,0:T(8,128)(2,1)S(1)} fusion(bf16[1024,7950]{0,1:T(8,128)(2,1)S(1)} %multiply_convert_fusion, bf16[1000,7950]{1,0:T(8,128)(2,1)} %param.8), kind=kOutput, calls=%fused_computation.7 | convolution fusion | flops 16282624000 | bytes 34229600 | tf_op jit(solution)/shard_map/dot_general | solution.py:32
  357.1 0.4 copy.37
  357.4 31.3 %all_to_all.27 = bf16[8,128,1000]{1,2,0:T(8,128)(2,1)S(1)} all-to-all(bf16[8,128,1000]{1,2,0:T(8,128)(2,1)S(1)} %bitcast.17), channel_id=1, replica_groups=mesh['sens'=8,'layer'=16] {'sens'}, dimensions={0} | all-to-all | bytes 4096000 | tf_op jit(solution)/shard_map/all_to_all | solution.py:27
  388.8 0.4 reduce_sum.41
  389.2 0.0 all-gather.3.cloned.1.call-done
  389.2 20.6 %reshape.36 = bf16[7800,1000]{1,0:T(8,128)(2,1)} reshape(bf16[8,975,1000]{2,1,0:T(8,128)(2,1)} %all-gather.3.cloned.1.call-done) | data formatting | bytes 31200000
  409.8 9.3 %convolution_convert_fusion = bf16[128,7800]{0,1:T(8,128)(2,1)} fusion(bf16[128,1000]{0,1:T(8,128)(2,1)S(1)} %reduce_sum.41, bf16[7800,1000]{1,0:T(8,128)(2,1)} %reshape.36), kind=kOutput, calls=%fused_computation.3 | convolution fusion | flops 1997798400 | bytes 17852800 | tf_op jit(solution)/shard_map/dot_general | solution.py:32
  419.1 2.9 copy.32
  422.0 29.9 %all_to_all.28 = bf16[16,8,7800]{2,1,0:T(8,128)(2,1)S(1)} all-to-all(bf16[16,8,7800]{2,1,0:T(8,128)(2,1)S(1)} %bitcast.18), channel_id=1, replica_groups=mesh['sens'=8,'layer'=16] {'layer'}, dimensions={0} | all-to-all | bytes 3993600 | tf_op jit(solution)/shard_map/all_to_all | solution.py:27
  451.9 1.0 convert_reduce_fusion
  (5 shorter events, 0.1 us)
Async XLA Ops:
  6.5 382.6 %all-gather.3.cloned.1.call-start = ((), (), s32[]{:S(2)}) async-start(), calls=%async_computation.5 | async-start | bytes 17989632 | tf_op jit(solution)/shard_map/all_gather | solution.py:68
  27.6 253.4 %all-to-all-start = ((bf16[16,64,7950]{2,1,0:T(8,128)(2,1)}), bf16[16,64,7950]{2,1,0:T(8,128)(2,1)}, u32[]{:S(2)}, u32[]{:S(2)}) async-start(bf16[16,64,7950]{2,1,0:T(8,128)(2,1)} %stack.2), calls=%async_computation | async-start | bytes 33030144 | tf_op jit(solution)/shard_map/all_to_all | solution.py:58
  291.8 25.8 %all-to-all-start.1 = ((bf16[8,1024,12]{1,2,0:T(8,128)(2,1)}), bf16[8,1024,12]{1,2,0:T(8,128)(2,1)S(1)}, u32[]{:S(2)}, u32[]{:S(2)}) async-start(bf16[8,1024,12]{1,2,0:T(8,128)(2,1)} %broadcast_in_dim.4), calls=%async_computation.1 | async-start | bytes 524288 | tf_op jit(solution)/shard_map/all_to_all | solution.py:11
Sparse Core Ops, SparseCore 0:
  9.0 84.3 all-gather.2
